TPU v7x, 128 devices: a whole 4x4x4 slice. The times are simulated.
128 devices in a mesh: row: 8 (over y, z_lo), col: 16 (over x, z_hi, core).
Axes of the slice: x: 4, y: 4, z: 4 (z_hi: 2, z_lo: 2; z = z_hi * 2 + z_lo), core: 2. Of those that a mesh axis runs over, the one named last changes fastest.
Arguments:
- eigvecs: float32 [512, 65536], P(('col', 'row')), may hold values from -6 to 6
- row_map: int32 [65536], replicated, may hold values from 0 to 65535, as said below
- reflectors: float32 [16, 512, 65536], P(None, 'col', 'row'), may hold values from -0.0234375 to 0.0234375
- panel_factor: float32 [2, 512, 512], replicated, may hold values from -4 to 4
- owners: int32 [16], replicated, may hold values from 0 to 15, each once
Outputs:
- back_vectors: float32 [512, 65536], P('col', 'row')
Inputs may be any that keep to these rules, and one draw needn't show every extreme that they name: row_map is a permutation of 0 to 65535 that moves aligned blocks of 64 rows whole, keeping the order inside a block. owners is a permutation; only its first 2 entries are read, so only those slots of reflectors are used.
All inputs are finite; a program needn't handle non-finite values.
Results may differ from a plain program's by a relative error of at most 0.0001.
Values sent between devices are 32-bit elements; how exact they have to be, the bound alone decides.
A program may use at most 128 MiB of HBM per device.

v0:
```python
import jax
import jax.numpy as jnp
from jax import lax
from jax.sharding import PartitionSpec as P

PANELS = 2
NB = 64


def from_everyone(x, axis):
    copies = jnp.broadcast_to(x, (lax.axis_size(axis), *x.shape))
    return lax.all_to_all(copies, axis, split_axis=0, concat_axis=0, tiled=True)


def taken_together(x, axis):
    return from_everyone(x, axis).sum(axis=0)


def hdot(left, right):
    return jnp.dot(left, right, precision=lax.Precision.HIGHEST, preferred_element_type=jnp.float32)


def per_device(eigvecs, row_map, reflectors, panel_factor, owners):
    row_count = lax.axis_size("row")
    eig_local = eigvecs.shape[0]
    total_rows = eigvecs.shape[1]
    local_rows = total_rows // row_count
    block_count = total_rows // NB
    block_index = row_map.reshape(block_count, NB)[:, 0] // NB
    blocked = eigvecs.reshape(eig_local, block_count, NB)
    ordered = jnp.take(blocked, block_index, axis=1).reshape(eig_local, row_count, local_rows)
    arrived = lax.all_to_all(ordered, "row", split_axis=1, concat_axis=0, tiled=True)
    current = arrived.reshape(eig_local * row_count, local_rows)
    for panel in range(PANELS):
        vectors = lax.all_gather(reflectors[owners[panel]], "col", axis=0, tiled=True)
        upper = jnp.triu(panel_factor[panel])
        project = taken_together(hdot(current, vectors.T), "row")
        scaled = hdot(project, upper.T)
        current = current - hdot(scaled, vectors)
    return current


def solution(mesh):
    placed = (P(("col", "row"), None), P(), P(None, "col", "row"), P(), P())
    return jax.shard_map(
        per_device, mesh=mesh, in_specs=placed, out_specs=P("col", "row"), check_vma=False
    )
```

profile of v0, /device:TPU:0, one launch (start us, length us, event | category | flops | bytes accessed | tf_op | source)
XLA Modules:
  0.0 297.6 jit_solution(3470367636473523635)
XLA Ops:
  6.5 0.0 all-gather.5.cloned.1.call-start
  6.5 1.3 fusion.26
  11.5 3.0 %constant_dynamic-slice_fusion = (f32[1,32,8192]{2,1,0:T(8,128)}, f32[1,32,8192]{2,1,0:T(8,128)}) fusion(f32[16,32,8192]{2,1,0:T(8,128)} %param.7, s32[]{:T(128)S(6)} %select_n.36, s32[]{:T(128)S(6)} %select_n.34), kind=kLoop, calls=%fused_computation.34 | loop fusion | bytes 4194312 | tf_op jit(solution)/shard_map/dynamic_slice | solution.py:35
  14.5 0.0 all-gather.5.cloned.1.call-update
  14.5 0.0 all-gather.7.cloned.1.call-start
  14.6 0.7 all-gather.7.cloned.1.call-update
  15.3 3.5 %reshape.21 = f32[4,1024,64]{2,1,0:T(8,128)} reshape(f32[4,65536]{1,0:T(4,128)} %param.5) | data formatting | bytes 2097152 | tf_op jit(solution)/shard_map/reshape | solution.py:30
  18.8 2.9 copy.15
  21.8 1.1 reshape.20
  22.9 0.5 and_reduce_fusion
  23.4 0.2 reduce.1
  23.6 7.9 %gather_fusion = f32[1024,4,64]{2,1,0:T(4,128)} fusion(f32[4,1024,64]{2,0,1:T(4,128)S(1)} %copy.15, s32[1024]{0:T(1024)S(1)} %broadcast_clamp_fusion), kind=kCustom, calls=%fused_computation | custom fusion | bytes 2101248 | tf_op jit(solution)/shard_map/jit(_take)/gather | solution.py:31
  31.6 1.7 copy.16
  33.3 0.7 gather.7
  33.9 0.2 broadcast_in_dim.28
  34.2 0.2 broadcast_in_dim.29
  34.4 0.1 broadcast_select_fusion
  34.5 0.7 copy.17
  35.2 21.1 %all_to_all.25 = f32[4,8,8192]{2,0,1:T(4,128)S(1)} all-to-all(f32[4,8,8192]{2,0,1:T(4,128)S(1)} %copy.17), channel_id=1, replica_groups=mesh['row'=8,'col'=16] {'row'}, dimensions={1} | all-to-all | bytes 2097152 | tf_op jit(solution)/shard_map/all_to_all | solution.py:32
  56.3 0.4 reshape.22
  56.6 0.0 copy-start
  56.6 70.3 %all-gather.5.cloned.1.call-done = f32[1,512,8192]{2,1,0:T(8,128)} async-done(((f32[1,32,8192]{2,1,0:T(8,128)}), f32[1,512,8192]{2,1,0:T(8,128)}) %all-gather.5.cloned.1.call-update) | async-done | bytes 16777232 | tf_op jit(solution)/shard_map/all_gather | solution.py:35
  126.9 18.1 %fusion.6 = f32[32,512]{1,0:T(8,128)S(1)} fusion(f32[32,8192]{1,0:T(8,128)S(1)} %reshape.22, f32[1,512,8192]{2,1,0:T(8,128)} %all-gather.5.cloned.1.call-done), kind=kOutput, calls=%fused_computation.7 | convolution fusion | flops 1610612736 | bytes 17891328 | tf_op jit(solution)/shard_map/dot_general | solution.py:20
  145.1 0.9 broadcast_in_dim.32
  146.0 4.4 %all-to-all-start.1 = ((f32[8,32,512]{2,1,0:T(8,128)}), f32[8,32,512]{2,1,0:T(8,128)}, u32[]{:S(2)}, u32[]{:S(2)}) async-start(f32[8,32,512]{2,1,0:T(8,128)} %broadcast_in_dim.32), calls=%async_computation.1 | async-start | bytes 1048576 | tf_op jit(solution)/shard_map/all_to_all | solution.py:12
  150.3 10.0 %all-to-all-done.1 = f32[8,32,512]{2,1,0:T(8,128)} async-done(((f32[8,32,512]{2,1,0:T(8,128)}), f32[8,32,512]{2,1,0:T(8,128)}, u32[]{:S(2)}, u32[]{:S(2)}) %all-to-all-start.1) | async-done | bytes 524320 | tf_op jit(solution)/shard_map/all_to_all | solution.py:12
  160.3 1.1 reduce_sum.18
  161.4 0.0 copy-done
  161.4 1.2 fusion.15
  162.6 13.1 %fusion.8 = f32[32,8192]{1,0:T(8,128)S(1)} fusion(f32[32,8192]{1,0:T(8,128)S(1)} %reshape.22, f32[32,512]{1,0:T(8,128)S(1)} %fusion.15, f32[1,512,8192]{2,1,0:T(8,128)} %all-gather.5.cloned.1.call-done), kind=kOutput, calls=%fused_computation.9 | convolution fusion | flops 1610874880 | bytes 18939904 | tf_op jit(solution)/shard_map/dot_general | solution.py:20
  175.7 65.9 %all-gather.7.cloned.1.call-done = f32[1,512,8192]{2,1,0:T(8,128)} async-done(((f32[1,32,8192]{2,1,0:T(8,128)}), f32[1,512,8192]{2,1,0:T(8,128)}) %all-gather.7.cloned.1.call-update) | async-done | bytes 16777232 | tf_op jit(solution)/shard_map/all_gather | solution.py:35
  241.6 18.1 %fusion.2 = f32[32,512]{1,0:T(8,128)S(1)} fusion(f32[32,8192]{1,0:T(8,128)S(1)} %fusion.8, f32[1,512,8192]{2,1,0:T(8,128)} %all-gather.7.cloned.1.call-done), kind=kOutput, calls=%fused_computation.3 | convolution fusion | flops 1610612736 | bytes 17891328 | tf_op jit(solution)/shard_map/dot_general | solution.py:20
  259.7 0.1 broadcast_in_dim.34
  259.8 14.3 %all_to_all.26 = f32[8,32,512]{2,1,0:T(8,128)S(1)} all-to-all(f32[8,32,512]{2,1,0:T(8,128)S(1)} %broadcast_in_dim.34), channel_id=1, replica_groups=mesh['row'=8,'col'=16] {'row'}, dimensions={0} | all-to-all | bytes 1048576 | tf_op jit(solution)/shard_map/all_to_all | solution.py:12
  274.2 2.4 fusion.14
  276.5 14.2 %fusion.11 = f32[32,8192]{1,0:T(8,128)} fusion(f32[32,8192]{1,0:T(8,128)S(1)} %fusion.8, f32[32,512]{1,0:T(8,128)S(1)} %fusion.14, f32[1,512,8192]{2,1,0:T(8,128)} %all-gather.7.cloned.1.call-done), kind=kOutput, calls=%fused_computation.10 | convolution fusion | flops 1610874880 | bytes 18939904 | tf_op jit(solution)/shard_map/dot_general | solution.py:20
  (3 shorter events, 0.0 us)
Async XLA Ops:
  6.5 120.4 %all-gather.5.cloned.1.call-start = ((), (), s32[]{:S(2)}) async-start(), calls=%async_computation.3 | async-start | bytes 17825792 | tf_op jit(solution)/shard_map/all_gather | solution.py:35
  14.5 227.1 %all-gather.7.cloned.1.call-start = ((), (), s32[]{:S(2)}) async-start(), calls=%async_computation.4 | async-start | bytes 17825792 | tf_op jit(solution)/shard_map/all_gather | solution.py:35
  56.6 104.8 %copy-start = (f32[2,512,512]{2,1,0:T(8,128)S(1)}, f32[2,512,512]{2,1,0:T(8,128)}, u32[]{:S(2)}) copy-start(f32[2,512,512]{2,1,0:T(8,128)} %param.8) | copy-start | bytes 6291460
  146.0 14.4 %all-to-all-start.1 = ((f32[8,32,512]{2,1,0:T(8,128)}), f32[8,32,512]{2,1,0:T(8,128)}, u32[]{:S(2)}, u32[]{:S(2)}) async-start(f32[8,32,512]{2,1,0:T(8,128)} %broadcast_in_dim.32), calls=%async_computation.1 | async-start | bytes 1048576 | tf_op jit(solution)/shard_map/all_to_all | solution.py:12
Sparse Core Ops, SparseCore 0:
  14.6 112.2 all-gather.4
  129.3 112.2 all-gather.6
where the time goes:
time: 298 us
  waiting for transfers between devices  147 us (49%)
  matrix products  67.1 us (23%)
  blocking collectives  35.4 us (12%)
  local copies, waits for them, and re-layouts  24.7 us (8%)
  between operations  17.1 us (6%)
  starting transfers between devices  4.43 us (1%)
    all_gather x2, waiting for transfers between devices, per_device(): lax.all_gather(reflectors[owners[panel]], 'col', axis=0, tiled=True)  136 us
    dot_general x6, matrix products, hdot(): jnp.dot(left, right, precision=lax.Precision.HIGHEST, preferred_element_t...  67.1 us
    all_to_all x1, blocking collectives, per_device(): lax.all_to_all(ordered, 'row', split_axis=1, concat_axis=0, tiled=True)  21.1 us
    all_to_all x1, blocking collectives, from_everyone(): return lax.all_to_all(copies, axis, split_axis=0, concat_axis=0, tiled=True)  14.3 us
    gather x3, local copies, waits for them, and re-layouts, per_device(): jnp.take(blocked, block_index, axis=1)  10.3 us
    all_to_all x1, waiting for transfers between devices, from_everyone(): return lax.all_to_all(copies, axis, split_axis=0, concat_axis=0, tiled=True)  9.99 us
    reshape x2, local copies, waits for them, and re-layouts, per_device(): blocked = eigvecs.reshape(eig_local, block_count, NB)  6.48 us
  transfers between devices with their start and end apart: 3, of which 3 were waited for; matrix products, arithmetic and copies ran while one was open for 18% of the time, Pallas kernels for 0%

commit v1 on v0

--- a/solution.py
+++ b/solution.py
@@ -1,3 +1,4 @@
+import functools
 import jax
 import jax.numpy as jnp
 from jax import lax
@@ -5,6 +6,22 @@
 
 PANELS = 2
 NB = 64
+
+
+def post_runs_on_mesh(local_block, across):
+    before = jnp.concatenate(
+        jax.lax.all_to_all(
+            jnp.stack([local_block for _ in range(jax.lax.axis_size(across))]),
+            across,
+            split_axis=0,
+            concat_axis=0,
+        ),
+        axis=0,
+    )
+    return before
+
+
+supply_all_edges_in = functools.partial(post_runs_on_mesh, across="col")
 
 
 def from_everyone(x, axis):
@@ -32,7 +49,7 @@
     arrived = lax.all_to_all(ordered, "row", split_axis=1, concat_axis=0, tiled=True)
     current = arrived.reshape(eig_local * row_count, local_rows)
     for panel in range(PANELS):
-        vectors = lax.all_gather(reflectors[owners[panel]], "col", axis=0, tiled=True)
+        vectors = supply_all_edges_in(reflectors[owners[panel]])
         upper = jnp.triu(panel_factor[panel])
         project = taken_together(hdot(current, vectors.T), "row")
         scaled = hdot(project, upper.T)

time: 298 us -> 697 us (2.34)
  waiting for transfers between devices: 147 us -> 535 us
  starting transfers between devices: 4.43 us -> 22.6 us
  local copies, waits for them, and re-layouts: 24.7 us -> 38.3 us
  between operations: 17.1 us -> 3.91 us
  blocking collectives: 35.4 us -> 25.4 us
    all_to_all x1 -> x3, waiting for transfers between devices: 9.99 us -> 535 us  [the longest x2 525 us: post_runs_on_mesh(): jax.lax.all_to_all(jnp.stack([local_block for _ in range(jax.lax.axis_siz...]
    all_gather x2 -> x0, waiting for transfers between devices: 136 us -> none  [per_device(): lax.all_gather(reflectors[owners[panel]], 'col', axis=0, tiled=True)]
    all_to_all x1 -> x0, blocking collectives: 21.1 us -> none  [per_device(): lax.all_to_all(ordered, 'row', split_axis=1, concat_axis=0, tiled=True)]
    all_to_all x1 -> x3, starting transfers between devices: 4.38 us -> 22.6 us  [the longest x2 16.7 us: post_runs_on_mesh(): jax.lax.all_to_all(jnp.stack([local_block for _ in range(jax.lax.axis_siz...]
    another operation x0 -> x2, local copies, waits for them, and re-layouts: none -> 15.5 us  [post_runs_on_mesh(): jnp.stack([local_block for _ in range(jax.lax.axis_size(across))])]
    all_to_all x1 -> x2, blocking collectives: 14.3 us -> 25.4 us  [from_everyone(): return lax.all_to_all(copies, axis, split_axis=0, concat_axis=0, tiled=True)]
  transfers between devices with their start and end apart: 3 -> 3, of which waited for: 3 -> 3; matrix products, arithmetic and copies ran while one was open for 18% -> 3% of each run, Pallas kernels for 0% -> 0%
where the time goes in v1:
time: 697 us; the launch traced here: 694 us
  waiting for transfers between devices  535 us (77%)
  matrix products  67.1 us (10%)
  local copies, waits for them, and re-layouts  38.3 us (5%)
  blocking collectives  25.4 us (4%)
  starting transfers between devices  22.6 us (3%)
    all_to_all x2, waiting for transfers between devices, post_runs_on_mesh(): jax.lax.all_to_all(jnp.stack([local_block for _ in range(jax.lax.axis_siz...  525 us
    dot_general x6, matrix products, hdot(): jnp.dot(left, right, precision=lax.Precision.HIGHEST, preferred_element_t...  67.1 us
    all_to_all x2, blocking collectives, from_everyone(): return lax.all_to_all(copies, axis, split_axis=0, concat_axis=0, tiled=True)  25.4 us
    all_to_all x2, starting transfers between devices, post_runs_on_mesh(): jax.lax.all_to_all(jnp.stack([local_block for _ in range(jax.lax.axis_siz...  16.7 us
    another operation x2, local copies, waits for them, and re-layouts, post_runs_on_mesh(): jnp.stack([local_block for _ in range(jax.lax.axis_size(across))])  15.5 us
  transfers between devices with their start and end apart: 3, of which 3 were waited for; matrix products, arithmetic and copies ran while one was open for 3% of the time, Pallas kernels for 0%

profile of v1, /device:TPU:0, one launch (start us, length us, event | category | flops | bytes accessed | tf_op | source)
XLA Modules:
  0.0 694.3 jit_solution(96758718015251292)
XLA Ops:
  0.0 0.0 copy-start.1
  0.0 1.1 reshape.28
  1.1 0.5 and_reduce_fusion
  1.6 0.2 reduce.1
  1.9 3.6 reshape.29
  5.4 2.9 copy.15
  8.4 8.0 %gather_fusion = f32[1024,4,64]{2,1,0:T(4,128)} fusion(f32[4,1024,64]{2,0,1:T(4,128)S(1)} %copy.15, s32[1024]{0:T(1024)S(1)} %broadcast_clamp_fusion), kind=kCustom, calls=%fused_computation | custom fusion | bytes 2101248 | tf_op jit(solution)/shard_map/jit(_take)/gather | solution.py:48
  16.3 1.7 copy.16
  18.1 0.7 gather.7
  18.7 0.2 broadcast_in_dim.28
  18.9 0.2 broadcast_in_dim.29
  19.2 0.1 broadcast_select_fusion
  19.3 1.6 copy.17
  20.9 5.9 all-to-all-start
  26.8 0.0 copy-done.1
  26.9 0.7 fusion.12
  31.3 1.7 dynamic-slice_bitcast_fusion
  33.0 9.8 %all-to-all-done = f32[4,8,8192]{2,0,1:T(4,128)S(1)} async-done(((f32[4,8,8192]{2,0,1:T(4,128)}), f32[4,8,8192]{2,0,1:T(4,128)S(1)}, u32[]{:S(2)}, u32[]{:S(2)}) %all-to-all-start) | async-done | bytes 1048608 | tf_op jit(solution)/shard_map/all_to_all | solution.py:49
  42.8 7.7 %stack.6 = f32[16,32,8192]{2,1,0:T(8,128)} broadcast(f32[32,8192]{1,0:T(8,128)S(1)} %get-tuple-element.8), dimensions={1,2} | broadcast | bytes 17825792 | tf_op jit(solution)/shard_map/stack | solution.py:14
  50.5 7.5 %all-to-all-start.1 = ((f32[16,32,8192]{2,1,0:T(8,128)}), f32[16,32,8192]{2,1,0:T(8,128)}, u32[]{:S(2)}, u32[]{:S(2)}) async-start(f32[16,32,8192]{2,1,0:T(8,128)} %stack.6), calls=%async_computation.1 | async-start | bytes 33554432 | tf_op jit(solution)/shard_map/all_to_all | solution.py:13
  58.0 0.4 reshape.30
  58.4 270.0 %all-to-all-done.1 = f32[16,32,8192]{2,1,0:T(8,128)} async-done(((f32[16,32,8192]{2,1,0:T(8,128)}), f32[16,32,8192]{2,1,0:T(8,128)}, u32[]{:S(2)}, u32[]{:S(2)}) %all-to-all-start.1) | async-done | bytes 16777248 | tf_op jit(solution)/shard_map/all_to_all | solution.py:13
  328.3 18.1 %fusion.13 = f32[32,512]{1,0:T(8,128)S(1)} fusion(f32[32,8192]{1,0:T(8,128)S(1)} %reshape.30, f32[512,8192]{1,0:T(8,128)} %bitcast.5), kind=kOutput, calls=%fused_computation.31 | convolution fusion | flops 1610612736 | bytes 17891328 | tf_op jit(solution)/shard_map/dot_general | solution.py:37
  346.5 0.1 broadcast_in_dim.32
  346.5 13.2 %all_to_all.35 = f32[8,32,512]{2,1,0:T(8,128)} all-to-all(f32[8,32,512]{2,1,0:T(8,128)S(1)} %broadcast_in_dim.32), channel_id=1, replica_groups=mesh['row'=8,'col'=16] {'row'}, dimensions={0} | all-to-all | bytes 1048576 | tf_op jit(solution)/shard_map/all_to_all | solution.py:29
  359.7 7.7 %stack.7 = f32[16,32,8192]{2,1,0:T(8,128)} broadcast(f32[32,8192]{1,0:T(8,128)S(1)} %get-tuple-element.7), dimensions={1,2} | broadcast | bytes 17825792 | tf_op jit(solution)/shard_map/stack | solution.py:14
  367.4 0.0 copy-start
  367.4 9.2 %all-to-all-start.3 = ((f32[16,32,8192]{2,1,0:T(8,128)}), f32[16,32,8192]{2,1,0:T(8,128)}, u32[]{:S(2)}, u32[]{:S(2)}) async-start(f32[16,32,8192]{2,1,0:T(8,128)} %stack.7), calls=%async_computation.3 | async-start | bytes 33554432 | tf_op jit(solution)/shard_map/all_to_all | solution.py:13
  376.6 1.1 reduce_sum.18
  377.7 0.0 copy-done
  377.7 1.1 fusion.1
  378.8 13.2 %convolution_subtract_fusion.1 = f32[32,8192]{1,0:T(8,128)S(1)} fusion(f32[32,8192]{1,0:T(8,128)S(1)} %reshape.30, f32[32,512]{1,0:T(8,128)S(1)} %fusion.1, f32[512,8192]{1,0:T(8,128)} %bitcast.5), kind=kOutput, calls=%fused_computation.2 | convolution fusion | flops 1610874880 | bytes 18939904 | tf_op jit(solution)/shard_map/dot_general | solution.py:37
  392.0 255.2 %all-to-all-done.3 = f32[16,32,8192]{2,1,0:T(8,128)} async-done(((f32[16,32,8192]{2,1,0:T(8,128)}), f32[16,32,8192]{2,1,0:T(8,128)}, u32[]{:S(2)}, u32[]{:S(2)}) %all-to-all-start.3) | async-done | bytes 16777248 | tf_op jit(solution)/shard_map/all_to_all | solution.py:13
  647.2 18.1 %fusion.14 = f32[32,512]{1,0:T(8,128)S(1)} fusion(f32[32,8192]{1,0:T(8,128)S(1)} %convolution_subtract_fusion.1, f32[512,8192]{1,0:T(8,128)} %bitcast.9), kind=kOutput, calls=%fused_computation.32 | convolution fusion | flops 1610612736 | bytes 17891328 | tf_op jit(solution)/shard_map/dot_general | solution.py:37
  665.4 0.1 broadcast_in_dim.34
  665.4 12.2 %all_to_all.36 = f32[8,32,512]{2,1,0:T(8,128)S(1)} all-to-all(f32[8,32,512]{2,1,0:T(8,128)S(1)} %broadcast_in_dim.34), channel_id=1, replica_groups=mesh['row'=8,'col'=16] {'row'}, dimensions={0} | all-to-all | bytes 1048576 | tf_op jit(solution)/shard_map/all_to_all | solution.py:29
  677.7 2.4 fusion
  680.1 14.2 %convolution_subtract_fusion = f32[32,8192]{1,0:T(8,128)} fusion(f32[32,8192]{1,0:T(8,128)S(1)} %convolution_subtract_fusion.1, f32[32,512]{1,0:T(8,128)S(1)} %fusion, f32[512,8192]{1,0:T(8,128)} %bitcast.9), kind=kOutput, calls=%fused_computation.1 | convolution fusion | flops 1610874880 | bytes 18939904 | tf_op jit(solution)/shard_map/dot_general | solution.py:37
  (3 shorter events, 0.0 us)
Async XLA Ops:
  0.0 26.8 %copy-start.1 = (s32[16]{0:T(128)S(1)}, s32[16]{0:T(128)}, u32[]{:S(2)}) copy-start(s32[16]{0:T(128)} %param.9) | copy-start | bytes 196
  20.9 21.8 %all-to-all-start = ((f32[4,8,8192]{2,0,1:T(4,128)}), f32[4,8,8192]{2,0,1:T(4,128)S(1)}, u32[]{:S(2)}, u32[]{:S(2)}) async-start(f32[4,8,8192]{2,0,1:T(4,128)} %copy.17), calls=%async_computation | async-start | bytes 2097152 | tf_op jit(solution)/shard_map/all_to_all | solution.py:49
  50.5 277.8 %all-to-all-start.1 = ((f32[16,32,8192]{2,1,0:T(8,128)}), f32[16,32,8192]{2,1,0:T(8,128)}, u32[]{:S(2)}, u32[]{:S(2)}) async-start(f32[16,32,8192]{2,1,0:T(8,128)} %stack.6), calls=%async_computation.1 | async-start | bytes 33554432 | tf_op jit(solution)/shard_map/all_to_all | solution.py:13
  367.4 10.3 %copy-start = (f32[2,512,512]{2,1,0:T(8,128)S(1)}, f32[2,512,512]{2,1,0:T(8,128)}, u32[]{:S(2)}) copy-start(f32[2,512,512]{2,1,0:T(8,128)} %param.8) | copy-start | bytes 6291460
  367.4 279.8 %all-to-all-start.3 = ((f32[16,32,8192]{2,1,0:T(8,128)}), f32[16,32,8192]{2,1,0:T(8,128)}, u32[]{:S(2)}, u32[]{:S(2)}) async-start(f32[16,32,8192]{2,1,0:T(8,128)} %stack.7), calls=%async_computation.3 | async-start | bytes 33554432 | tf_op jit(solution)/shard_map/all_to_all | solution.py:13
